TPU v7x, 32 devices: a whole 2x2x4 slice. The times are simulated.
32 devices in a mesh: sub: 8 (over y, x, core), coarse: 4 (over z).
Axes of the slice: x: 2, y: 2, z: 4, core: 2. Of those that a mesh axis runs over, the one named last changes fastest.
Arguments:
- right_side: float32 [8, 4, 128, 128], P('sub', 'coarse'), may hold values from -150 to 150
- diagonal: float32 [8, 4, 128, 128], P('sub', 'coarse'), may hold values from 2 to 8
- cell_link: float32 [8, 4, 128, 128], P('sub', 'coarse'), may hold values from 0.2 to 0.9
- block_inverse: float32 [8, 4, 128, 128, 128], P('sub', 'coarse'), may hold values from -1 to 1
- coupling: float32 [8, 4, 4, 128, 128], P('sub', 'coarse'), may hold values from -0.26516503 to 0.26516503
- coarse_basis: float32 [8, 4, 128, 128], P('sub', 'coarse'), may hold values from -6 to 6
- coarse_inverse: float32 [512, 512], P('coarse'), may hold values from -0.25 to 0.25
- partner: int32 [8, 4], P('sub'), may hold values from 0 to 7, as said below
- margin_width: int32 [8, 4], P('sub'), may hold values from 4 to 8, as said below
- margin_blocks: int32 [8, 4, 4, 8], P('sub', 'coarse'), may hold values from 0 to 127
- aggregate: int32 [8, 4, 128], P('sub', 'coarse'), may hold values from 0 to 511, as said below
Outputs:
- solution: float32 [8, 4, 128, 128], P('sub', 'coarse')
Inputs may be any that keep to these rules, and one draw needn't show every extreme that they name: partner[s, r] differs from s, partner[partner[s, r], r] = s, and the 4 partners of one subdomain are distinct. margin_width[partner[s, r], r] = margin_width[s, r]; every colour round has a pair with width 8. `margin_blocks`: entries with w >= margin_width[s, r] are not used. aggregate[s, c, b] lies in (s * 4 + c) * 16 to (s * 4 + c + 1) * 16 - 1, and every one of these 16 aggregates has a block of part [s, c].
All inputs are finite; a program needn't handle non-finite values.
Results may differ from a plain program's by a relative error of at most 0.0003.
Values sent between devices are 32-bit elements; how exact they have to be, the bound alone decides.
No kernel may reach another device: no remote copies, remote signals or barrier semaphores. Data moves between devices by JAX's collectives and lax.ppermute only.
A program may use at most 64 MiB of HBM per device.

v0:
```python
import jax
import jax.numpy as jnp
from jax import lax
from jax.sharding import PartitionSpec as P

BS = 128
BPD = 128
AGG_DEV = 16
ITERS = 4


def givens_solve(columns, beta):
    steps_count = len(columns)
    cosines = []
    sines = []
    side_terms = [beta] + [jnp.zeros_like(beta) for unused in range(steps_count)]
    triangle = []
    for column_id in range(steps_count):
        column = list(columns[column_id])
        for row_id in range(column_id):
            upper = column[row_id]
            lower = column[row_id + 1]
            column[row_id] = cosines[row_id] * upper + sines[row_id] * lower
            column[row_id + 1] = cosines[row_id] * lower - sines[row_id] * upper
        upper = column[column_id]
        lower = column[column_id + 1]
        radius = jnp.sqrt(upper * upper + lower * lower)
        cosine = upper / radius
        sine_value = lower / radius
        column[column_id] = radius
        cosines.append(cosine)
        sines.append(sine_value)
        side_terms[column_id + 1] = -sine_value * side_terms[column_id]
        side_terms[column_id] = cosine * side_terms[column_id]
        triangle.append(column)
    weights = [None] * steps_count
    for column_id in reversed(range(steps_count)):
        running = side_terms[column_id]
        for later_col in range(column_id + 1, steps_count):
            running = running - triangle[later_col][column_id] * weights[later_col]
        weights[column_id] = running / triangle[column_id][column_id]
    return weights


def on_device(
    right_side,
    diagonal,
    cell_link,
    block_inverse,
    coupling,
    coarse_basis,
    coarse_inverse,
    partner,
    margin_width,
    margin_blocks,
    aggregate,
):
    highest = lax.Precision.HIGHEST
    block_count = right_side.shape[2]
    unknowns = right_side.shape[3]
    factor = (BS * BPD / AGG_DEV) ** (-0.5)
    inverse_blocks = block_inverse[0, 0]
    couplings = coupling[0, 0]
    basis_local = coarse_basis[0, 0]
    diagonal_local = diagonal[0, 0]
    link_local = cell_link[0, 0]
    paired = partner[0]
    widths = margin_width[0]
    blocks = margin_blocks[0, 0]
    member_of = aggregate[0, 0]
    aggregate_count = coarse_inverse.shape[1]
    member_table = (member_of[:, None] == jnp.arange(aggregate_count)[None, :]).astype(jnp.float32)
    rounds = blocks.shape[0]
    widest = blocks.shape[1]
    target = (blocks.reshape(-1)[:, None] == jnp.arange(block_count)[None, :]).astype(jnp.float32)
    live_mask = (jnp.arange(widest)[None, :] < widths[:, None]).astype(jnp.float32)

    def margin(values):
        outgoing = jnp.take(values, blocks.reshape(-1), axis=0).reshape(rounds, widest, unknowns)
        pieces = []
        for round_id in range(rounds):
            gathered = lax.all_gather(outgoing[round_id], "sub", axis=0, tiled=True)
            pieces.append(lax.dynamic_slice_in_dim(gathered, paired[round_id] * widest, widest, 0))
        incoming = jnp.stack(pieces)
        mapped = (
            jnp.einsum("rij,rwj->rwi", couplings, incoming, precision=highest)
            * live_mask[:, :, None]
        )
        return jnp.einsum(
            "kb,ki->bi", target, mapped.reshape(rounds * widest, unknowns), precision=highest
        )

    def squared_norm(values):
        return lax.psum(jnp.sum(values * values), ("sub", "coarse"))

    start_vector = right_side[0, 0]
    directions = []
    columns = []
    beta = jnp.sqrt(squared_norm(start_vector))
    basis_list = [start_vector / beta]
    for krylov_step in range(ITERS):
        current = basis_list[-1]
        inner = jnp.sum(basis_local * current, axis=1)
        restricted = lax.psum(
            jnp.dot(inner, member_table, precision=highest) * factor, ("sub", "coarse")
        )
        local_part = jnp.einsum(
            "bij,bj->bi", inverse_blocks, current + margin(current), precision=highest
        )
        coarse_part = jnp.dot(coarse_inverse, restricted, precision=highest)
        coarse_full = lax.all_gather(coarse_part, "coarse", axis=0, tiled=True)
        prolonged = jnp.dot(member_table, coarse_full, precision=highest)
        direction = local_part + prolonged[:, None] * basis_local
        directions.append(direction)
        flat_line = direction.reshape(-1)
        link_line = link_local.reshape(-1)
        zero_pad = jnp.zeros((1,), jnp.float32)
        ahead_terms = jnp.concatenate([flat_line[1:], zero_pad]) * link_line
        behind_terms = jnp.concatenate([zero_pad, (link_line * flat_line)[:-1]])
        product = (
            diagonal_local * direction
            - (ahead_terms + behind_terms).reshape(direction.shape)
            - margin(direction)
        )
        projected = lax.psum(
            jnp.stack([jnp.sum(vector * product) for vector in basis_list]), ("sub", "coarse")
        )
        for position in range(len(basis_list)):
            product = product - projected[position] * basis_list[position]
        norm_new = jnp.sqrt(squared_norm(product))
        columns.append([projected[position] for position in range(len(basis_list))] + [norm_new])
        basis_list.append(product / norm_new)
    weights = givens_solve(columns, beta)
    solution = weights[0] * directions[0]
    for position in range(1, ITERS):
        solution = solution + weights[position] * directions[position]
    return solution.reshape(right_side.shape)


def solution(mesh):
    placed = (
        P("sub", "coarse", None, None),
        P("sub", "coarse", None, None),
        P("sub", "coarse", None, None),
        P("sub", "coarse", None, None, None),
        P("sub", "coarse", None, None, None),
        P("sub", "coarse", None, None),
        P("coarse", None),
        P("sub", None),
        P("sub", None),
        P("sub", "coarse", None, None),
        P("sub", "coarse", None),
    )
    return jax.shard_map(
        on_device,
        mesh=mesh,
        in_specs=placed,
        out_specs=P("sub", "coarse", None, None),
        check_vma=False,
    )
```

profile of v0, /device:TPU:0, one launch (start us, length us, event | category | flops | bytes accessed | tf_op | source)
XLA Modules:
  0.0 958.9 jit_solution(15861982066872133460)
XLA Ops:
  2.3 42.2 %psum.91 = f32[]{:T(128)} all-reduce(f32[]{:T(128)} %multiply_reduce_fusion.14), channel_id=1, replica_groups=mesh['sub'=8,'coarse'=4] {'sub','coarse'}, use_global_device_ids=true, to_apply=%region_1.0 | all-reduce | flops 1 | bytes 8 | tf_op jit(solution)/shard_map/psum | solution.py:94
  46.9 10.0 %all_gather.108 = f32[64,128]{1,0:T(8,128)S(1)} all-gather(f32[8,128]{1,0:T(8,128)S(1)} %get-tuple-element.63), channel_id=1, replica_groups=mesh['sub'=8,'coarse'=4] {'sub'}, dimensions={0}, use_global_device_ids=true | all-gather | bytes 36864 | tf_op jit(solution)/shard_map/all_gather | solution.py:82
  67.9 9.1 all_gather.110
  87.8 15.4 %fusion.6 = f32[128,1,128]{2,1,0:T(1,128)S(1)} fusion(f32[128,128,1]{1,2,0:T(1,128)S(1)} %bitcast.355, f32[1,1,128,128,128]{4,3,2,1,0:T(8,128)} %param.16), kind=kOutput, calls=%fused_computation.14 | convolution fusion | flops 25165824 | bytes 8519680 | tf_op jit(solution)/shard_map/bij,bj->bi/dot_general | solution.py:107
  103.5 39.4 %psum.92 = f32[512]{0:T(512)S(1)} all-reduce(f32[512]{0:T(512)S(1)} %broadcast_multiply_fusion.3), channel_id=1, replica_groups=mesh['sub'=8,'coarse'=4] {'sub','coarse'}, use_global_device_ids=true, to_apply=%region_3.5 | all-reduce | flops 512 | bytes 4096 | tf_op jit(solution)/shard_map/psum | solution.py:104
  143.1 9.8 %all-gather = f32[4,1,128]{2,1,0:T(1,128)S(1)} all-gather(f32[1,1,128]{2,1,0:T(1,128)S(1)} %convolution_bitcast_fusion.7), channel_id=1, replica_groups=mesh['sub'=8,'coarse'=4] {'coarse'}, dimensions={0}, use_global_device_ids=true | all-gather | bytes 2560 | tf_op jit(solution)/shard_map/all_gather | solution.py:111
  153.9 9.8 %all_gather.113 = f32[64,128]{1,0:T(8,128)S(1)} all-gather(f32[8,128]{1,0:T(8,128)S(1)} %get-tuple-element.59), channel_id=1, replica_groups=mesh['sub'=8,'coarse'=4] {'sub'}, dimensions={0}, use_global_device_ids=true | all-gather | bytes 36864 | tf_op jit(solution)/shard_map/all_gather | solution.py:82
  163.8 9.1 all_gather.114
  180.9 9.1 all_gather.116
  191.5 37.8 %psum.93 = f32[]{:T(128)} all-reduce(f32[]{:T(128)} %get-tuple-element.80), channel_id=1, replica_groups=mesh['sub'=8,'coarse'=4] {'sub','coarse'}, use_global_device_ids=true, to_apply=%region_5.7 | all-reduce | flops 1 | bytes 8 | tf_op jit(solution)/shard_map/psum | solution.py:125
  230.6 41.2 %psum.94 = f32[]{:T(128)} all-reduce(f32[]{:T(128)} %multiply_reduce_fusion.12), channel_id=1, replica_groups=mesh['sub'=8,'coarse'=4] {'sub','coarse'}, use_global_device_ids=true, to_apply=%region_7.9 | all-reduce | flops 1 | bytes 8 | tf_op jit(solution)/shard_map/psum | solution.py:94
  274.0 10.1 %all_gather.117 = f32[64,128]{1,0:T(8,128)S(1)} all-gather(f32[8,128]{1,0:T(8,128)S(1)} %get-tuple-element.55), channel_id=1, replica_groups=mesh['sub'=8,'coarse'=4] {'sub'}, dimensions={0}, use_global_device_ids=true | all-gather | bytes 36864 | tf_op jit(solution)/shard_map/all_gather | solution.py:82
  311.1 15.4 %fusion.4 = f32[128,1,128]{2,1,0:T(1,128)S(1)} fusion(f32[128,128,1]{1,2,0:T(1,128)S(1)} %bitcast.356, f32[1,1,128,128,128]{4,3,2,1,0:T(8,128)} %param.16), kind=kOutput, calls=%fused_computation.12 | convolution fusion | flops 25165824 | bytes 8519680 | tf_op jit(solution)/shard_map/bij,bj->bi/dot_general | solution.py:107
  326.8 37.7 %psum.95 = f32[512]{0:T(512)S(1)} all-reduce(f32[512]{0:T(512)S(1)} %broadcast_multiply_fusion.2), channel_id=1, replica_groups=mesh['sub'=8,'coarse'=4] {'sub','coarse'}, use_global_device_ids=true, to_apply=%region_9.11 | all-reduce | flops 512 | bytes 4096 | tf_op jit(solution)/shard_map/psum | solution.py:104
  364.7 9.6 %all-gather.1 = f32[4,1,128]{2,1,0:T(1,128)S(1)} all-gather(f32[1,1,128]{2,1,0:T(1,128)S(1)} %convolution_bitcast_fusion.5), channel_id=1, replica_groups=mesh['sub'=8,'coarse'=4] {'coarse'}, dimensions={0}, use_global_device_ids=true | all-gather | bytes 2560 | tf_op jit(solution)/shard_map/all_gather | solution.py:111
  375.4 9.8 %all_gather.122 = f32[64,128]{1,0:T(8,128)S(1)} all-gather(f32[8,128]{1,0:T(8,128)S(1)} %get-tuple-element.51), channel_id=1, replica_groups=mesh['sub'=8,'coarse'=4] {'sub'}, dimensions={0}, use_global_device_ids=true | all-gather | bytes 36864 | tf_op jit(solution)/shard_map/all_gather | solution.py:82
  413.5 37.6 %psum.96 = f32[2]{0:T(128)S(1)} all-reduce(f32[2]{0:T(128)S(1)} %pad_maximum_fusion.8), channel_id=1, replica_groups=mesh['sub'=8,'coarse'=4] {'sub','coarse'}, use_global_device_ids=true, to_apply=%region_12.14 | all-reduce | flops 2 | bytes 16 | tf_op jit(solution)/shard_map/psum | solution.py:125
  453.6 41.7 %psum.97 = f32[]{:T(128)} all-reduce(f32[]{:T(128)} %get-tuple-element.21), channel_id=1, replica_groups=mesh['sub'=8,'coarse'=4] {'sub','coarse'}, use_global_device_ids=true, to_apply=%region_14.16 | all-reduce | flops 1 | bytes 8 | tf_op jit(solution)/shard_map/psum | solution.py:94
  496.8 10.1 %all_gather.126 = f32[64,128]{1,0:T(8,128)S(1)} all-gather(f32[8,128]{1,0:T(8,128)S(1)} %get-tuple-element.47), channel_id=1, replica_groups=mesh['sub'=8,'coarse'=4] {'sub'}, dimensions={0}, use_global_device_ids=true | all-gather | bytes 36864 | tf_op jit(solution)/shard_map/all_gather | solution.py:82
  533.0 15.4 %fusion.2 = f32[128,1,128]{2,1,0:T(1,128)S(1)} fusion(f32[128,128,1]{1,2,0:T(1,128)S(1)} %bitcast.357, f32[1,1,128,128,128]{4,3,2,1,0:T(8,128)} %param.16), kind=kOutput, calls=%fused_computation.10 | convolution fusion | flops 25165824 | bytes 8519680 | tf_op jit(solution)/shard_map/bij,bj->bi/dot_general | solution.py:107
  548.6 37.7 %psum.98 = f32[512]{0:T(512)S(1)} all-reduce(f32[512]{0:T(512)S(1)} %broadcast_multiply_fusion.1), channel_id=1, replica_groups=mesh['sub'=8,'coarse'=4] {'sub','coarse'}, use_global_device_ids=true, to_apply=%region_16.18 | all-reduce | flops 512 | bytes 4096 | tf_op jit(solution)/shard_map/psum | solution.py:104
  586.5 9.6 %all-gather.2 = f32[4,1,128]{2,1,0:T(1,128)S(1)} all-gather(f32[1,1,128]{2,1,0:T(1,128)S(1)} %convolution_bitcast_fusion.3), channel_id=1, replica_groups=mesh['sub'=8,'coarse'=4] {'coarse'}, dimensions={0}, use_global_device_ids=true | all-gather | bytes 2560 | tf_op jit(solution)/shard_map/all_gather | solution.py:111
  597.2 9.8 %all_gather.131 = f32[64,128]{1,0:T(8,128)S(1)} all-gather(f32[8,128]{1,0:T(8,128)S(1)} %get-tuple-element.43), channel_id=1, replica_groups=mesh['sub'=8,'coarse'=4] {'sub'}, dimensions={0}, use_global_device_ids=true | all-gather | bytes 36864 | tf_op jit(solution)/shard_map/all_gather | solution.py:82
  637.2 37.6 %psum.99 = f32[3]{0:T(128)S(1)} all-reduce(f32[3]{0:T(128)S(1)} %pad_maximum_fusion.9), channel_id=1, replica_groups=mesh['sub'=8,'coarse'=4] {'sub','coarse'}, use_global_device_ids=true, to_apply=%region_20.22 | all-reduce | flops 3 | bytes 24 | tf_op jit(solution)/shard_map/psum | solution.py:125
  677.9 40.7 %psum.100 = f32[]{:T(128)} all-reduce(f32[]{:T(128)} %get-tuple-element.17), channel_id=1, replica_groups=mesh['sub'=8,'coarse'=4] {'sub','coarse'}, use_global_device_ids=true, to_apply=%region_22.24 | all-reduce | flops 1 | bytes 8 | tf_op jit(solution)/shard_map/psum | solution.py:94
  720.0 10.0 %all_gather.135 = f32[64,128]{1,0:T(8,128)S(1)} all-gather(f32[8,128]{1,0:T(8,128)S(1)} %get-tuple-element.39), channel_id=1, replica_groups=mesh['sub'=8,'coarse'=4] {'sub'}, dimensions={0}, use_global_device_ids=true | all-gather | bytes 36864 | tf_op jit(solution)/shard_map/all_gather | solution.py:82
  757.1 15.4 %fusion = f32[128,1,128]{2,1,0:T(1,128)S(1)} fusion(f32[128,128,1]{1,2,0:T(1,128)S(1)} %bitcast.358, f32[1,1,128,128,128]{4,3,2,1,0:T(8,128)} %param.16), kind=kOutput, calls=%fused_computation.8 | convolution fusion | flops 25165824 | bytes 8519680 | tf_op jit(solution)/shard_map/bij,bj->bi/dot_general | solution.py:107
  772.7 37.7 %psum.101 = f32[512]{0:T(512)S(1)} all-reduce(f32[512]{0:T(512)S(1)} %broadcast_multiply_fusion), channel_id=1, replica_groups=mesh['sub'=8,'coarse'=4] {'sub','coarse'}, use_global_device_ids=true, to_apply=%region_24.26 | all-reduce | flops 512 | bytes 4096 | tf_op jit(solution)/shard_map/psum | solution.py:104
  810.6 9.6 %all-gather.3 = f32[4,1,128]{2,1,0:T(1,128)S(1)} all-gather(f32[1,1,128]{2,1,0:T(1,128)S(1)} %convolution_bitcast_fusion.1), channel_id=1, replica_groups=mesh['sub'=8,'coarse'=4] {'coarse'}, dimensions={0}, use_global_device_ids=true | all-gather | bytes 2560 | tf_op jit(solution)/shard_map/all_gather | solution.py:111
  821.3 9.8 %all_gather.140 = f32[64,128]{1,0:T(8,128)S(1)} all-gather(f32[8,128]{1,0:T(8,128)S(1)} %get-tuple-element.35), channel_id=1, replica_groups=mesh['sub'=8,'coarse'=4] {'sub'}, dimensions={0}, use_global_device_ids=true | all-gather | bytes 36864 | tf_op jit(solution)/shard_map/all_gather | solution.py:82
  860.6 37.6 %psum.102 = f32[4]{0:T(128)S(1)} all-reduce(f32[4]{0:T(128)S(1)} %pad_maximum_fusion.10), channel_id=1, replica_groups=mesh['sub'=8,'coarse'=4] {'sub','coarse'}, use_global_device_ids=true, to_apply=%region_29.31 | all-reduce | flops 4 | bytes 32 | tf_op jit(solution)/shard_map/psum | solution.py:125
  908.5 41.8 %psum.103 = f32[]{:T(128)} all-reduce(f32[]{:T(128)} %multiply_reduce_fusion), channel_id=1, replica_groups=mesh['sub'=8,'coarse'=4] {'sub','coarse'}, use_global_device_ids=true, to_apply=%region_31.33 | all-reduce | flops 1 | bytes 8 | tf_op jit(solution)/shard_map/psum | solution.py:94
  (151 shorter events, 221.4 us)
Async XLA Ops:
  0.0 87.0 %copy-start = (f32[1,1,4,128,128]{4,3,2,1,0:T(8,128)S(1)}, f32[1,1,4,128,128]{4,3,2,1,0:T(8,128)}, u32[]{:S(2)}) copy-start(f32[1,1,4,128,128]{4,3,2,1,0:T(8,128)} %param.17) | copy-start | bytes 786436
  0.0 153.1 %copy-start.1 = (f32[1,1,128,128]{3,2,1,0:T(8,128)S(1)}, f32[1,1,128,128]{3,2,1,0:T(8,128)}, u32[]{:S(2)}) copy-start(f32[1,1,128,128]{3,2,1,0:T(8,128)} %param.18) | copy-start | bytes 196612
  0.0 103.2 %copy-start.5 = (s32[1,1,128]{2,1,0:T(1,128)S(1)}, s32[1,1,128]{2,1,0:T(1,128)}, u32[]{:S(2)}) copy-start(s32[1,1,128]{2,1,0:T(1,128)} %param.23) | copy-start | bytes 1540
  0.0 142.9 %copy-start.2 = (f32[128,512]{1,0:T(8,128)S(1)}, f32[128,512]{1,0:T(8,128)}, u32[]{:S(2)}) copy-start(f32[128,512]{1,0:T(8,128)} %param.19) | copy-start | bytes 786436
  0.0 190.4 %copy-start.3 = (f32[1,1,128,128]{3,2,1,0:T(8,128)S(1)}, f32[1,1,128,128]{3,2,1,0:T(8,128)}, u32[]{:S(2)}) copy-start(f32[1,1,128,128]{3,2,1,0:T(8,128)} %param.15) | copy-start | bytes 196612
  0.0 190.5 %copy-start.4 = (f32[1,1,128,128]{3,2,1,0:T(8,128)S(1)}, f32[1,1,128,128]{3,2,1,0:T(8,128)}, u32[]{:S(2)}) copy-start(f32[1,1,128,128]{3,2,1,0:T(8,128)} %param.14) | copy-start | bytes 196612
where the time goes:
time: 971 us; the launch traced here: 959 us
  blocking collectives  835 us (86%)
  matrix products  73.9 us (8%)
  other arithmetic  21.1 us (2%)
  between operations  20.1 us (2%)
    all_gather x32, blocking collectives, margin(): gathered = lax.all_gather(outgoing[round_id], 'sub', axis=0, tiled=True)  286 us
    psum x5, blocking collectives, squared_norm(): return lax.psum(jnp.sum(values * values), ('sub', 'coarse'))  208 us
    psum x4, blocking collectives, on_device(): lax.psum(jnp.dot(inner, member_table, precision=highest) * factor, ('sub'...  152 us
    psum x4, blocking collectives, on_device(): lax.psum(jnp.stack([jnp.sum(vector * product) for vector in basis_list]),...  151 us
    dot_general x4, matrix products, on_device(): jnp.einsum('bij,bj->bi', inverse_blocks, current + margin(current), preci...  61.5 us
    all_gather x4, blocking collectives, on_device(): coarse_full = lax.all_gather(coarse_part, 'coarse', axis=0, tiled=True)  38.7 us

commit v1 on v0

--- a/solution.py
+++ b/solution.py
@@ -108,7 +108,14 @@
             "bij,bj->bi", inverse_blocks, current + margin(current), precision=highest
         )
         coarse_part = jnp.dot(coarse_inverse, restricted, precision=highest)
-        coarse_full = lax.all_gather(coarse_part, "coarse", axis=0, tiled=True)
+        peers = lax.axis_size("coarse")
+        route = [(i, (i + 1) % peers) for i in range(peers)]
+        parts = [coarse_part]
+        for far in range(1, peers):
+            parts = [lax.ppermute(parts[0], "coarse", route), *parts]
+        whole = jnp.concatenate(parts, axis=0)
+        turn = (lax.axis_index("coarse") + 1) * parts[-1].shape[0]
+        coarse_full = jnp.roll(whole, turn, axis=0)
         prolonged = jnp.dot(member_table, coarse_full, precision=highest)
         direction = local_part + prolonged[:, None] * basis_local
         directions.append(direction)

time: 971 us -> 937 us (0.965)
  matrix products: 73.9 us -> 13.6 us
  blocking collectives: 835 us -> 797 us
  waiting for transfers between devices: 0 us -> 25 us
  other arithmetic: 21.1 us -> 42.5 us
  starting transfers between devices: 0 us -> 11.7 us
    dot_general x4 -> x0, matrix products: 61.5 us -> none  [on_device(): jnp.einsum('bij,bj->bi', inverse_blocks, current + margin(current), preci...]
    all_gather x4 -> x0, blocking collectives: 38.7 us -> none  [on_device(): coarse_full = lax.all_gather(coarse_part, 'coarse', axis=0, tiled=True)]
    ppermute x0 -> x12, waiting for transfers between devices: none -> 25 us  [on_device(): parts = [lax.ppermute(parts[0], 'coarse', route), *parts]]
    unnamed x0 -> x4, other arithmetic: none -> 22.5 us
    ppermute x0 -> x12, starting transfers between devices: none -> 11.7 us  [on_device(): parts = [lax.ppermute(parts[0], 'coarse', route), *parts]]
  transfers between devices with their start and end apart: 0 -> 12, of which waited for: 0 -> 6; matrix products, arithmetic and copies ran while one was open for 0% -> 4% of each run, Pallas kernels for 0% -> 0%
where the time goes in v1:
time: 937 us; the launch traced here: 925 us
  blocking collectives  797 us (85%)
  other arithmetic  42.5 us (5%)
  waiting for transfers between devices  25 us (3%)
  between operations  21.1 us (2%)
  local copies, waits for them, and re-layouts  14.2 us (2%)
  matrix products  13.6 us (1%)
  starting transfers between devices  11.7 us (1%)
    all_gather x32, blocking collectives, margin(): gathered = lax.all_gather(outgoing[round_id], 'sub', axis=0, tiled=True)  279 us
    psum x5, blocking collectives, squared_norm(): return lax.psum(jnp.sum(values * values), ('sub', 'coarse'))  210 us
    psum x4, blocking collectives, on_device(): lax.psum(jnp.dot(inner, member_table, precision=highest) * factor, ('sub'...  158 us
    psum x4, blocking collectives, on_device(): lax.psum(jnp.stack([jnp.sum(vector * product) for vector in basis_list]),...  150 us
    ppermute x12, waiting for transfers between devices, on_device(): parts = [lax.ppermute(parts[0], 'coarse', route), *parts]  25 us
    unnamed x4, other arithmetic  22.5 us
  transfers between devices with their start and end apart: 12, of which 6 were waited for; matrix products, arithmetic and copies ran while one was open for 4% of the time, Pallas kernels for 0%

profile of v1, /device:TPU:0, one launch (start us, length us, event | category | flops | bytes accessed | tf_op | source)
XLA Modules:
  0.0 925.2 jit_solution(2926567250989327984)
XLA Ops:
  2.5 42.3 %psum.91 = f32[]{:T(128)} all-reduce(f32[]{:T(128)} %multiply_reduce_fusion.14), channel_id=1, replica_groups=mesh['sub'=8,'coarse'=4] {'sub','coarse'}, use_global_device_ids=true, to_apply=%region_1.0 | all-reduce | flops 1 | bytes 8 | tf_op jit(solution)/shard_map/psum | solution.py:94
  47.3 40.3 %psum.92 = f32[512]{0:T(512)S(1)} all-reduce(f32[512]{0:T(512)S(1)} %broadcast_multiply_fusion.3), channel_id=1, replica_groups=mesh['sub'=8,'coarse'=4] {'sub','coarse'}, use_global_device_ids=true, to_apply=%region_3.5 | all-reduce | flops 512 | bytes 4096 | tf_op jit(solution)/shard_map/psum | solution.py:104
  95.8 9.8 %all_gather.96 = f32[64,128]{1,0:T(8,128)S(1)} all-gather(f32[8,128]{1,0:T(8,128)S(1)} %get-tuple-element.64), channel_id=1, replica_groups=mesh['sub'=8,'coarse'=4] {'sub'}, dimensions={0}, use_global_device_ids=true | all-gather | bytes 36864 | tf_op jit(solution)/shard_map/all_gather | solution.py:82
  105.6 9.0 all_gather.99
  122.7 9.0 all_gather.97
  158.3 9.0 all_gather.103
  175.4 9.0 all_gather.101
  186.2 37.1 %psum.93 = f32[]{:T(128)} all-reduce(f32[]{:T(128)} %get-tuple-element.81), channel_id=1, replica_groups=mesh['sub'=8,'coarse'=4] {'sub','coarse'}, use_global_device_ids=true, to_apply=%region_5.8 | all-reduce | flops 1 | bytes 8 | tf_op jit(solution)/shard_map/psum | solution.py:132
  224.6 41.8 %psum.94 = f32[]{:T(128)} all-reduce(f32[]{:T(128)} %multiply_reduce_fusion.12), channel_id=1, replica_groups=mesh['sub'=8,'coarse'=4] {'sub','coarse'}, use_global_device_ids=true, to_apply=%region_7.10 | all-reduce | flops 1 | bytes 8 | tf_op jit(solution)/shard_map/psum | solution.py:94
  268.1 39.6 %psum.95 = f32[512]{0:T(512)S(1)} all-reduce(f32[512]{0:T(512)S(1)} %broadcast_multiply_fusion.2), channel_id=1, replica_groups=mesh['sub'=8,'coarse'=4] {'sub','coarse'}, use_global_device_ids=true, to_apply=%region_9.12 | all-reduce | flops 512 | bytes 4096 | tf_op jit(solution)/shard_map/psum | solution.py:104
  311.3 9.8 %all_gather.104 = f32[64,128]{1,0:T(8,128)S(1)} all-gather(f32[8,128]{1,0:T(8,128)S(1)} %get-tuple-element.56), channel_id=1, replica_groups=mesh['sub'=8,'coarse'=4] {'sub'}, dimensions={0}, use_global_device_ids=true | all-gather | bytes 36864 | tf_op jit(solution)/shard_map/all_gather | solution.py:82
  329.3 9.0 all_gather.106
  361.2 9.0 all_gather.108
  378.4 9.0 all_gather.110
  398.8 39.1 %psum.96 = f32[2]{0:T(128)S(1)} all-reduce(f32[2]{0:T(128)S(1)} %pad_maximum_fusion.8), channel_id=1, replica_groups=mesh['sub'=8,'coarse'=4] {'sub','coarse'}, use_global_device_ids=true, to_apply=%region_12.15 | all-reduce | flops 2 | bytes 16 | tf_op jit(solution)/shard_map/psum | solution.py:132
  440.6 41.7 %psum.97 = f32[]{:T(128)} all-reduce(f32[]{:T(128)} %get-tuple-element.22), channel_id=1, replica_groups=mesh['sub'=8,'coarse'=4] {'sub','coarse'}, use_global_device_ids=true, to_apply=%region_14.17 | all-reduce | flops 1 | bytes 8 | tf_op jit(solution)/shard_map/psum | solution.py:94
  483.2 38.7 %psum.98 = f32[512]{0:T(512)S(1)} all-reduce(f32[512]{0:T(512)S(1)} %broadcast_multiply_fusion.1), channel_id=1, replica_groups=mesh['sub'=8,'coarse'=4] {'sub','coarse'}, use_global_device_ids=true, to_apply=%region_16.19 | all-reduce | flops 512 | bytes 4096 | tf_op jit(solution)/shard_map/psum | solution.py:104
  525.1 9.8 %all_gather.112 = f32[64,128]{1,0:T(8,128)S(1)} all-gather(f32[8,128]{1,0:T(8,128)S(1)} %get-tuple-element.48), channel_id=1, replica_groups=mesh['sub'=8,'coarse'=4] {'sub'}, dimensions={0}, use_global_device_ids=true | all-gather | bytes 36864 | tf_op jit(solution)/shard_map/all_gather | solution.py:82
  534.9 9.0 all_gather.115
  552.0 9.1 all_gather.113
  586.5 9.0 all_gather.119
  603.6 9.0 all_gather.117
  616.5 36.8 %psum.99 = f32[3]{0:T(128)S(1)} all-reduce(f32[3]{0:T(128)S(1)} %pad_maximum_fusion.9), channel_id=1, replica_groups=mesh['sub'=8,'coarse'=4] {'sub','coarse'}, use_global_device_ids=true, to_apply=%region_20.23 | all-reduce | flops 3 | bytes 24 | tf_op jit(solution)/shard_map/psum | solution.py:132
  656.6 41.6 %psum.100 = f32[]{:T(128)} all-reduce(f32[]{:T(128)} %get-tuple-element.18), channel_id=1, replica_groups=mesh['sub'=8,'coarse'=4] {'sub','coarse'}, use_global_device_ids=true, to_apply=%region_22.25 | all-reduce | flops 1 | bytes 8 | tf_op jit(solution)/shard_map/psum | solution.py:94
  699.1 39.6 %psum.101 = f32[512]{0:T(512)S(1)} all-reduce(f32[512]{0:T(512)S(1)} %broadcast_multiply_fusion), channel_id=1, replica_groups=mesh['sub'=8,'coarse'=4] {'sub','coarse'}, use_global_device_ids=true, to_apply=%region_24.27 | all-reduce | flops 512 | bytes 4096 | tf_op jit(solution)/shard_map/psum | solution.py:104
  741.9 9.8 %all_gather.120 = f32[64,128]{1,0:T(8,128)S(1)} all-gather(f32[8,128]{1,0:T(8,128)S(1)} %get-tuple-element.40), channel_id=1, replica_groups=mesh['sub'=8,'coarse'=4] {'sub'}, dimensions={0}, use_global_device_ids=true | all-gather | bytes 36864 | tf_op jit(solution)/shard_map/all_gather | solution.py:82
  759.9 9.0 all_gather.122
  768.9 8.3 all_gather.121
  796.2 9.0 all_gather.124
  813.3 9.0 all_gather.126
  835.0 36.8 %psum.102 = f32[4]{0:T(128)S(1)} all-reduce(f32[4]{0:T(128)S(1)} %pad_maximum_fusion.10), channel_id=1, replica_groups=mesh['sub'=8,'coarse'=4] {'sub','coarse'}, use_global_device_ids=true, to_apply=%region_29.32 | all-reduce | flops 4 | bytes 32 | tf_op jit(solution)/shard_map/psum | solution.py:132
  880.8 42.5 %psum.103 = f32[]{:T(128)} all-reduce(f32[]{:T(128)} %multiply_reduce_fusion), channel_id=1, replica_groups=mesh['sub'=8,'coarse'=4] {'sub','coarse'}, use_global_device_ids=true, to_apply=%region_31.34 | all-reduce | flops 1 | bytes 8 | tf_op jit(solution)/shard_map/psum | solution.py:94
  (213 shorter events, 212.8 us)
Async XLA Ops:
  0.0 131.7 %copy-start = (f32[1,1,4,128,128]{4,3,2,1,0:T(8,128)S(1)}, f32[1,1,4,128,128]{4,3,2,1,0:T(8,128)}, u32[]{:S(2)}) copy-start(f32[1,1,4,128,128]{4,3,2,1,0:T(8,128)} %param.19) | copy-start | bytes 786436
  0.0 149.1 %copy-start.4 = (s32[1,1,128]{2,1,0:T(1,128)S(1)}, s32[1,1,128]{2,1,0:T(1,128)}, u32[]{:S(2)}) copy-start(s32[1,1,128]{2,1,0:T(1,128)} %param.25) | copy-start | bytes 1540
  0.0 307.7 %copy-start.1 = (f32[128,512]{1,0:T(8,128)S(1)}, f32[128,512]{1,0:T(8,128)}, u32[]{:S(2)}) copy-start(f32[128,512]{1,0:T(8,128)} %param.21) | copy-start | bytes 786436
  0.0 143.7 %copy-start.3 = (f32[1,1,128,128]{3,2,1,0:T(8,128)S(1)}, f32[1,1,128,128]{3,2,1,0:T(8,128)}, u32[]{:S(2)}) copy-start(f32[1,1,128,128]{3,2,1,0:T(8,128)} %param.16) | copy-start | bytes 196612
  0.0 143.8 %copy-start.2 = (f32[1,1,128,128]{3,2,1,0:T(8,128)S(1)}, f32[1,1,128,128]{3,2,1,0:T(8,128)}, u32[]{:S(2)}) copy-start(f32[1,1,128,128]{3,2,1,0:T(8,128)} %param.17) | copy-start | bytes 196612
  88.9 49.4 %collective-permute-start = (f32[128]{0:T(128)S(1)}, f32[128]{0:T(128)S(1)}, u32[]{:S(2)}, u32[]{:S(2)}) collective-permute-start(f32[128]{0:T(128)S(1)} %convolution_bitcast_fusion.7), channel_id=1, source_target_pairs={{0,1},{1,2},{2,3},{3,0},{4,5},{5,6},{6,7},{7,4},{8,9},{9,10},{10,1... | collective-permute-start | bytes 1544 | tf_op jit(solution)/shard_map/ppermute | solution.py:115
  138.3 5.4 collective-permute-start.1
  143.7 5.3 collective-permute-start.2
  308.0 38.9 %collective-permute-start.3 = (f32[128]{0:T(128)S(1)}, f32[128]{0:T(128)S(1)}, u32[]{:S(2)}, u32[]{:S(2)}) collective-permute-start(f32[128]{0:T(128)S(1)} %convolution_bitcast_fusion.5), channel_id=1, source_target_pairs={{0,1},{1,2},{2,3},{3,0},{4,5},{5,6},{6,7},{7,4},{8,9},{9,10},{10,1... | collective-permute-start | bytes 1544 | tf_op jit(solution)/shard_map/ppermute | solution.py:115
  346.9 5.4 collective-permute-start.4
  352.3 7.8 collective-permute-start.5
  522.2 39.9 %collective-permute-start.6 = (f32[128]{0:T(128)S(1)}, f32[128]{0:T(128)S(1)}, u32[]{:S(2)}, u32[]{:S(2)}) collective-permute-start(f32[128]{0:T(128)S(1)} %convolution_bitcast_fusion.3), channel_id=1, source_target_pairs={{0,1},{1,2},{2,3},{3,0},{4,5},{5,6},{6,7},{7,4},{8,9},{9,10},{10,1... | collective-permute-start | bytes 1544 | tf_op jit(solution)/shard_map/ppermute | solution.py:115
  562.1 9.7 %collective-permute-start.7 = (f32[128]{0:T(128)S(1)}, f32[128]{0:T(128)S(1)}, u32[]{:S(2)}, u32[]{:S(2)}) collective-permute-start(f32[128]{0:T(128)S(1)} %collective-permute-done.6), channel_id=1, source_target_pairs={{0,1},{1,2},{2,3},{3,0},{4,5},{5,6},{6,7},{7,4},{8,9},{9,10},{10,1... | collective-permute-start | bytes 1544 | tf_op jit(solution)/shard_map/ppermute | solution.py:115
  571.8 5.4 collective-permute-start.8
  739.0 45.3 %collective-permute-start.9 = (f32[128]{0:T(128)S(1)}, f32[128]{0:T(128)S(1)}, u32[]{:S(2)}, u32[]{:S(2)}) collective-permute-start(f32[128]{0:T(128)S(1)} %convolution_bitcast_fusion.1), channel_id=1, source_target_pairs={{0,1},{1,2},{2,3},{3,0},{4,5},{5,6},{6,7},{7,4},{8,9},{9,10},{10,1... | collective-permute-start | bytes 1544 | tf_op jit(solution)/shard_map/ppermute | solution.py:115
  784.3 5.4 collective-permute-start.10
  789.7 5.3 collective-permute-start.11
